TPU v7x, 128 devices: a whole 4x4x4 slice. The times are simulated.
128 devices in a mesh: dp: 32 (over z, x, core), mp: 4 (over y).
Axes of the slice: x: 4, y: 4, z: 4, core: 2. Of those that a mesh axis runs over, the one named last changes fastest.
Arguments:
- hidden: bfloat16 [40960, 8192], P('dp', 'mp'), may hold values from -6 to 6
- rewards: float32 [256, 160], P('dp'), may hold values from -4 to 4
- lengths: int32 [256], P('dp'), may hold values from 1 to 160, as said below
- dest_shard: int32 [256], P('dp'), may hold values from 0 to 31, as said below
- source_owner: int32 [256], P('dp'), may hold values from 0 to 31, as said below
- pack_offset: int32 [256], P('dp'), may hold values from 0 to 639, as said below
- segment_ids: int32 [20480], P('dp'), may hold values from 0 to 7, as said below
- norm_gain: float32 [8192], replicated, may hold values from 0.5 to 1.5
- w_query: bfloat16 [8192, 4096], P(None, 'mp'), may hold values from -1 to 1
- w_key: bfloat16 [8192, 512], P(None, 'mp'), may hold values from -1 to 1
- w_value: bfloat16 [8192, 512], P(None, 'mp'), may hold values from -0.0625 to 0.0625
- value_head: float32 [8192], P('mp'), may hold values from -0.0625 to 0.0625
- folded_head: float32 [4096], P('mp'), may hold values from -0.09375 to 0.09375
Outputs:
- values: float32 [256, 160], P('dp')
- advantages: float32 [256, 160], P('dp')
Inputs may be any that keep to these rules, and one draw needn't show every extreme that they name: `lengths`: rows of a slot past its rollout's length are unused. Every critic shard holds a rollout of 160 rows. Some owner's 8 rollouts all have 160 rows. `dest_shard`: owner o packs its 8 rollouts on the shards o, o + 1, ..., o + 7, modulo the number of shards, one on each. `source_owner`: shard s packs one rollout from each of the owners s, s - 1, ..., s - 7, modulo the number of shards, in some order, agreeing with dest_shard. `pack_offset`: A shard's packed rollouts lie back to back in the order of their index, each with the length that lengths gives it, and fill all 640 rows. `segment_ids`: each packed row names the index of the packed rollout that holds it, as pack_offset and lengths lay them out.
All inputs are finite; a program needn't handle non-finite values.
Results may differ from a plain program's by a relative error of at most 0.007.
Values may be sent and summed in bfloat16 or wider, within the bound.
A program may use at most 192 MiB of HBM per device.

v0:
```python
import math
import jax
import jax.numpy as jnp
from jax import lax
from jax.sharding import PartitionSpec as P

HD = 128
EPSILON = 1e-05
DISCOUNT = 0.99
SMOOTHING = 0.95
ROPE_BASE = 500000.0


def passed_along(value, axis, by):
    length = lax.axis_size(axis)
    return lax.ppermute(value, axis, [(i, (i + by) % length) for i in range(length)])


def rotary(values_in, positions):
    half_width = values_in.shape[-1] // 2
    frequency = ROPE_BASE ** (-jnp.arange(half_width, dtype=jnp.float32) / half_width)
    angles = positions.astype(jnp.float32)[:, None] * frequency[None, :]
    cosine = jnp.cos(angles)[:, None, :]
    sine_part = jnp.sin(angles)[:, None, :]
    front_half = values_in[..., :half_width]
    back_half = values_in[..., half_width:]
    return jnp.concatenate(
        [front_half * cosine - back_half * sine_part, back_half * cosine + front_half * sine_part],
        axis=-1,
    )


def head_values(queries, keys_out, values_out, segments, positions, folded_head):
    row_count = queries.shape[0]
    kv_count = keys_out.shape[1] // HD
    group_size = queries.shape[1] // HD // kv_count
    query_rot = rotary(queries.reshape(row_count, kv_count * group_size, HD), positions).astype(
        jnp.bfloat16
    )
    query_rot = query_rot.reshape(row_count, kv_count, group_size, HD)
    key_rot = rotary(keys_out.reshape(row_count, kv_count, HD), positions).astype(jnp.bfloat16)
    value_rows = values_out.astype(jnp.bfloat16).reshape(row_count, kv_count, HD)
    scores = jnp.einsum(
        "qhgd,khd->hgqk", query_rot, key_rot, preferred_element_type=jnp.float32
    ) / math.sqrt(HD)
    allowed = (segments[:, None] == segments[None, :]) & (positions[:, None] >= positions[None, :])
    scores = jnp.where(allowed[None, None], scores, -1e30)
    row_max = jnp.max(scores, axis=-1, keepdims=True)
    exp_scores = jnp.where(allowed[None, None], jnp.exp(scores - row_max), 0.0)
    row_total = jnp.sum(exp_scores, axis=-1, keepdims=True)
    weights = (exp_scores / row_total).astype(jnp.bfloat16)
    attended = jnp.einsum("hgqk,khd->qhgd", weights, value_rows, preferred_element_type=jnp.float32)
    return jnp.sum(attended.reshape(row_count, -1) * folded_head[None, :], axis=1)


def local(
    hidden,
    rewards,
    lengths,
    dest_shard,
    source_owner,
    pack_offset,
    segment_ids,
    norm_gain,
    w_query,
    w_key,
    w_value,
    value_head,
    folded_head,
):
    shards = lax.axis_size("dp")
    shard_index = lax.axis_index("dp")
    rollouts = lengths.shape[0]
    slot_rows = rewards.shape[1]
    packed_rows = segment_ids.shape[0]
    slot_lanes = jnp.arange(rollouts, dtype=jnp.int32)

    def slot_for(shift_by):
        target = (shard_index + shift_by) % shards
        return jnp.sum(jnp.where(dest_shard == target, slot_lanes, 0))

    def outgoing(shift_by, source):
        return lax.dynamic_slice_in_dim(source, slot_for(shift_by) * slot_rows, slot_rows, 0)

    source_step = (shard_index - source_owner) % shards
    lane_match = segment_ids[:, None] == slot_lanes[None, :]
    row_step = jnp.sum(jnp.where(lane_match, source_step[None, :], 0), axis=1)
    row_offset = jnp.sum(jnp.where(lane_match, pack_offset[None, :], 0), axis=1)
    positions = jnp.arange(packed_rows, dtype=jnp.int32) - row_offset
    pick_rows = row_step * slot_rows + positions
    received = [outgoing(0, hidden)]
    for shift_by in range(1, rollouts):
        received.append(passed_along(outgoing(shift_by, hidden), "dp", shift_by))
    own_part = jnp.take(jnp.concatenate(received, axis=0), pick_rows, axis=0)
    packed = lax.all_gather(own_part, "mp", axis=1, tiled=True)
    packed_f = packed.astype(jnp.float32)
    row_scale = lax.rsqrt(jnp.mean(packed_f * packed_f, axis=1) + EPSILON)
    normed = (packed_f * row_scale[:, None] * norm_gain[None, :]).astype(jnp.bfloat16)
    queries = jnp.dot(normed, w_query, preferred_element_type=jnp.float32)
    keys_out = jnp.dot(normed, w_key, preferred_element_type=jnp.float32)
    values_out = jnp.dot(normed, w_value, preferred_element_type=jnp.float32)
    value_terms = head_values(queries, keys_out, values_out, segment_ids, positions, folded_head)
    value_terms = value_terms + jnp.sum(own_part.astype(jnp.float32) * value_head[None, :], axis=1)
    packed_values = lax.psum(value_terms, "mp")
    padded = jnp.concatenate([packed_values, jnp.zeros((slot_rows,), jnp.float32)])
    slot_values = jnp.zeros((rollouts, slot_rows), jnp.float32)
    for shift_by in range(rollouts):
        owner_now = (shard_index - shift_by) % shards
        j_index = jnp.sum(jnp.where(source_owner == owner_now, slot_lanes, 0))
        start_at = jnp.sum(jnp.where(slot_lanes == j_index, pack_offset, 0))
        arrived = lax.dynamic_slice_in_dim(padded, start_at, slot_rows, 0)
        if shift_by:
            arrived = passed_along(arrived, "dp", -shift_by)
        slot_values = jnp.where(
            (slot_lanes == slot_for(shift_by))[:, None], arrived[None, :], slot_values
        )
    step_ids = jnp.arange(slot_rows, dtype=jnp.int32)
    live_mask = step_ids[None, :] < lengths[:, None]
    values = jnp.where(live_mask, slot_values, 0.0)
    next_live = step_ids[None, :] + 1 < lengths[:, None]
    following = jnp.concatenate([values[:, 1:], jnp.zeros((rollouts, 1), jnp.float32)], axis=1)
    one_step = jnp.where(
        live_mask, rewards + DISCOUNT * jnp.where(next_live, following, 0.0) - values, 0.0
    )
    lag_matrix = (step_ids[:, None] - step_ids[None, :]).astype(jnp.float32)
    decay_table = jnp.where(
        lag_matrix >= 0, jnp.exp(lag_matrix * math.log(DISCOUNT * SMOOTHING)), 0.0
    )
    advantages = jnp.dot(one_step, decay_table, precision=lax.Precision.HIGHEST)
    return (values, advantages)


def solution(mesh):
    return jax.shard_map(
        local,
        mesh=mesh,
        in_specs=(
            P("dp", "mp"),
            P("dp", None),
            P("dp"),
            P("dp"),
            P("dp"),
            P("dp"),
            P("dp"),
            P(),
            P(None, "mp"),
            P(None, "mp"),
            P(None, "mp"),
            P("mp"),
            P("mp"),
        ),
        out_specs=(P("dp", None), P("dp", None)),
        check_vma=False,
    )
```

profile of v0, /device:TPU:1, one launch (start us, length us, event | category | flops | bytes accessed | tf_op | source)
XLA Modules:
  0.0 324.4 jit_solution(14331908132062440243)
XLA Ops:
  7.2 0.0 all-gather.2.cloned.1.call-start
  7.4 1.9 fusion.49
  14.4 3.8 %constant_dynamic-slice_fusion = (bf16[160,2048]{1,0:T(8,128)(2,1)S(1)}, bf16[160,2048]{1,0:T(8,128)(2,1)S(1)}, bf16[160,2048]{1,0:T(8,128)(2,1)S(1)}, bf16[160,...) fusion(bf16[1280,2048]{1,0:T(8,128)(2,1)} %param.13, ...), kind=kLoop, calls=%fused_computation.98 | loop fusion | bytes 10485792 | tf_op jit(solution)/shard_map/dynamic_slice | solution.py:83
  18.2 2.6 collective-permute-start
  20.8 1.2 collective-permute-start.1
  22.0 1.5 collective-permute-start.2
  23.5 1.9 collective-permute-start.3
  25.4 3.4 %collective-permute-start.4 = (bf16[160,2048]{1,0:T(8,128)(2,1)S(1)}, bf16[160,2048]{1,0:T(8,128)(2,1)S(1)}, u32[]{:S(2)}, u32[]{:S(2)}) collective-permute-start(bf16[160,2048]{1,0:T(8,128)(2,1)S(1)} %get-tuple-element.33), channel_id=1, source_target_pairs={{0,20},{4,24},{8,28},{12,32},{16,36},{20,40},{24,44},{28,48},{32,5... | collective-permute-start | bytes 1966088 | tf_op jit(solution)/shard_map/ppermute | solution.py:16
  28.8 0.1 select_reduce_fusion.1
  28.9 5.8 %collective-permute-done = bf16[160,2048]{1,0:T(8,128)(2,1)S(1)} collective-permute-done((bf16[160,2048]{1,0:T(8,128)(2,1)S(1)}, bf16[160,2048]{1,0:T(8,128)(2,1)S(1)}, u32[]{:S(2)}, u32[]{:S(2)}) %collective-permute-start) | collective-permute-done | bytes 655392 | tf_op jit(solution)/shard_map/ppermute | solution.py:16
  34.8 2.8 collective-permute-start.5
  37.6 0.9 constant_dynamic-update-slice_fusion.6
  38.5 14.7 %collective-permute-done.1 = bf16[160,2048]{1,0:T(8,128)(2,1)S(1)} collective-permute-done((bf16[160,2048]{1,0:T(8,128)(2,1)S(1)}, bf16[160,2048]{1,0:T(8,128)(2,1)S(1)}, u32[]{:S(2)}, u32[]{:S(2)}) %collective-permute-start.1) | collective-permute-done | bytes 655392 | tf_op jit(solution)/shard_map/ppermute | solution.py:16
  53.1 0.9 constant_dynamic-update-slice_fusion.5
  54.1 8.8 %collective-permute-done.2 = bf16[160,2048]{1,0:T(8,128)(2,1)S(1)} collective-permute-done((bf16[160,2048]{1,0:T(8,128)(2,1)S(1)}, bf16[160,2048]{1,0:T(8,128)(2,1)S(1)}, u32[]{:S(2)}, u32[]{:S(2)}) %collective-permute-start.2) | collective-permute-done | bytes 655392 | tf_op jit(solution)/shard_map/ppermute | solution.py:16
  62.8 0.9 constant_dynamic-update-slice_fusion.4
  63.8 35.7 %collective-permute-done.3 = bf16[160,2048]{1,0:T(8,128)(2,1)S(1)} collective-permute-done((bf16[160,2048]{1,0:T(8,128)(2,1)S(1)}, bf16[160,2048]{1,0:T(8,128)(2,1)S(1)}, u32[]{:S(2)}, u32[]{:S(2)}) %collective-permute-start.3) | collective-permute-done | bytes 655392 | tf_op jit(solution)/shard_map/ppermute | solution.py:16
  99.4 0.9 constant_dynamic-update-slice_fusion.3
  100.3 0.0 collective-permute-done.4
  100.4 0.9 constant_dynamic-update-slice_fusion.2
  101.3 7.6 %collective-permute-done.5 = bf16[160,2048]{1,0:T(8,128)(2,1)S(1)} collective-permute-done((bf16[160,2048]{1,0:T(8,128)(2,1)S(1)}, bf16[160,2048]{1,0:T(8,128)(2,1)S(1)}, u32[]{:S(2)}, u32[]{:S(2)}) %collective-permute-start.5) | collective-permute-done | bytes 655392 | tf_op jit(solution)/shard_map/ppermute | solution.py:16
  108.9 0.9 constant_dynamic-update-slice_fusion.1
  109.8 5.4 %collective-permute-done.6 = bf16[160,2048]{1,0:T(8,128)(2,1)S(1)} collective-permute-done((bf16[160,2048]{1,0:T(8,128)(2,1)S(1)}, bf16[160,2048]{1,0:T(8,128)(2,1)S(1)}, u32[]{:S(2)}, u32[]{:S(2)}) %collective-permute-start.6) | collective-permute-done | bytes 655392 | tf_op jit(solution)/shard_map/ppermute | solution.py:16
  115.1 0.9 constant_dynamic-update-slice_fusion
  116.0 10.1 %gather_fusion = bf16[640,2048]{1,0:T(8,128)(2,1)} fusion(bf16[1280,2048]{1,0:T(8,128)(2,1)} %constant_dynamic-update-slice_fusion, s32[1024]{0:T(1024)S(1)} %pad_clamp_fusion), kind=kCustom, calls=%fused_computation | custom fusion | bytes 5245440 | tf_op jit(solution)/shard_map/jit(_take)/gather | solution.py:94
  126.1 4.1 %multiply_reduce_fusion = (f32[640]{0:T(1024)S(1)}, bf16[640,2048]{1,0:T(8,128)(2,1)}) fusion(f32[2048]{0:T(1024)S(1)} %copy-done.6, bf16[640,2048]{1,0:T(8,128)(2,1)} %gather_fusion, pred[640]{0:T(1024)(128)(4,1)S(1)} %compare_and_fusion.1), kind=kLoop, calls=%fused_computation.13 | loop fusion | flops 5242240 | bytes 5254272 | tf_op jit(solution)/shard_map/reduce_sum | solution.py:103
  130.2 5.9 %fusion.58 = (s32[]{:T(128)}, s32[]{:T(128)}, s32[]{:T(128)}, s32[]{:T(128)}, s32[]{:T(128)}, /*index=5*/s32[]{:T(128)}, s32[]{:T(128)}, s32[]{:T(128)}) fusion(s32[8]{0:T(128)S(1)} %copy-done.7, s32[]{:T(128)} %get-tuple-element.67, s32[]{:T(128)} %get-tuple-element.66, s32[]{:T(128)} %get-tuple-element.65, s32[]{:T(128)} %get-tuple-element.64, ...), kind=kLoop, calls=%fused_computation.140 | loop fusion | flops 184 | bytes 96 | tf_op jit(solution)/shard_map/reduce_sum | solution.py:110
  151.1 1.3 iota_compare_fusion.3
  152.4 1.2 iota_compare_fusion.4
  153.6 1.1 iota_compare_fusion.5
  154.7 1.2 iota_compare_fusion.6
  155.9 1.2 iota_compare_fusion.7
  157.0 1.2 iota_compare_fusion.8
  158.2 0.6 iota_add_fusion
  158.8 1.1 compare_and_fusion
  159.9 2.0 multiply_cosine_fusion
  161.9 69.3 %all-gather.2.cloned.1.call-done = bf16[640,8192]{1,0:T(8,128)(2,1)} async-done(((bf16[640,2048]{1,0:T(8,128)(2,1)}), bf16[640,8192]{1,0:T(8,128)(2,1)}) %all-gather.2.cloned.1.call-update) | async-done | bytes 10485776 | tf_op jit(solution)/shard_map/all_gather | solution.py:95
  231.2 6.2 %fusion = f32[640]{0:T(1024)S(1)} fusion(bf16[640,8192]{1,0:T(8,128)(2,1)} %all-gather.2.cloned.1.call-done), kind=kLoop, calls=%fused_computation.3 | loop fusion | flops 15728000 | bytes 10488320 | tf_op jit(solution)/shard_map/reduce_sum | solution.py:97
  237.5 0.7 copy-done.2
  238.2 14.8 %convolution_bitcast_fusion = f32[80,8,8,128]{3,1,2,0:T(8,128)S(1)} fusion(bf16[8192,1024]{1,0:T(8,128)(2,1)} %param.21, bf16[640,8192]{1,0:T(8,128)(2,1)S(1)} %copy-done.2, f32[8192]{0:T(1024)} %param.20, f32[640]{0:T(1024)S(1)} %add_rsqrt_fusion), kind=kOutput, calls=%fused_computation.19 | convolution fusion | flops 10758389760 | bytes 29919744 | tf_op jit(solution)/shard_map/dot_general | solution.py:99
  253.0 0.6 copy.35
  253.6 0.8 fusion.86
  254.5 4.9 %convolution_bitcast_fusion.1 = f32[640,1,128]{0,2,1:T(8,128)} fusion(bf16[8192,128]{1,0:T(8,128)(2,1)S(1)} %copy-done, bf16[640,8192]{1,0:T(8,128)(2,1)S(1)} %copy-done.2, f32[8192]{0:T(1024)} %param.20, f32[640]{0:T(1024)S(1)} %add_rsqrt_fusion), kind=kOutput, calls=%fused_computation.25 | convolution fusion | flops 1363148800 | bytes 12945920 | tf_op jit(solution)/shard_map/dot_general | solution.py:100
  259.3 1.7 fusion.36
  261.1 2.1 subtract_convert_fusion
  263.2 6.4 %fusion.3 = (f32[8,640]{1,0:T(8,128)S(1)}, f32[640,640,8]{1,0,2:T(8,128)}) fusion(pred[640,640]{0,1:T(8,128)(4,1)S(1)} %copy-done.3, bf16[640,8,64]{2,0,1:T(8,128)(2,1)S(1)} %get-tuple-element.31, bf16[640,8,64]{2,0,1:T(8,128)(2,1)S(1)} %get-tuple-element.30, bf16[640,64]{0,1:T(8,128)(2,1)S(1)} %get-tuple-element.43, bf16[640,64]{0,1:T(8,128)(2,1)S(1)} %get-tuple-element.42), kind=kOutput, calls=%fused_computation.9 | convolution fusion | flops 851635200 | bytes 15011840 | tf_op jit(solution)/shard_map/qhgd,khd->hgqk/dot_general | solution.py:43
  269.6 7.8 %fusion.4 = f32[8,640]{1,0:T(8,128)S(1)} fusion(f32[640,640,8]{1,0,2:T(8,128)} %get-tuple-element.58, f32[8,640]{1,0:T(8,128)S(1)} %get-tuple-element.57, pred[640,640]{0,1:T(8,128)(4,1)S(1)} %copy-done.3), kind=kLoop, calls=%fused_computation.10 | loop fusion | flops 16378880 | bytes 13557760 | tf_op jit(solution)/shard_map/reduce_sum | solution.py:50
  277.5 14.9 %fusion.7 = f32[640]{0:T(1024)S(1)} fusion(f32[8,640]{1,0:T(8,128)S(1)} %fusion.4, f32[8,640]{1,0:T(8,128)S(1)} %get-tuple-element.57, f32[640,640,8]{1,0,2:T(8,128)} %get-tuple-element.58, pred[640,640]{0,1:T(8,128)(4,1)S(1)} %copy-done.3, f32[8,128]{1,0:T(8,128)S(1)} %bitcast.51, bf16[8192,128]{1,0:T(8,128)(2,1)} %param.23, ...), kind=kOutput, calls=%fused_computation.15 | convolution fusion | flops 2223062528 | bytes 26182656 | tf_op jit(solution)/shard_map/hgqk,khd->qhgd/dot_general | solution.py:52
  292.4 7.2 %psum.7 = f32[640]{0:T(1024)S(1)} all-reduce(f32[640]{0:T(1024)S(1)} %add.252), channel_id=1, replica_groups=mesh['dp'=32,'mp'=4] {'mp'}, use_global_device_ids=true, to_apply=%region_15.16 | all-reduce | flops 640 | bytes 5120 | tf_op jit(solution)/shard_map/psum | solution.py:104
  299.7 0.1 pad_dynamic-slice_fusion.7
  299.8 3.0 collective-permute-start.13
  302.7 5.0 %collective-permute-start.12 = (f32[160]{0:T(256)S(1)}, f32[160]{0:T(256)S(1)}, u32[]{:S(2)}, u32[]{:S(2)}) collective-permute-start(f32[160]{0:T(256)S(1)} %get-tuple-element.51), channel_id=1, source_target_pairs={{0,120},{4,124},{8,0},{12,4},{16,8},{20,12},{24,16},{28,20},{32,24... | collective-permute-start | bytes 1928 | tf_op jit(solution)/shard_map/ppermute | solution.py:16
  307.7 0.6 iota_compare_fusion.9
  308.3 0.9 collective-permute-start.11
  309.2 0.3 collective-permute-start.10
  309.5 3.1 collective-permute-start.9
  312.6 0.5 collective-permute-start.8
  313.1 0.8 collective-permute-start.7
  313.9 0.6 iota_compare_fusion.10
  314.6 1.7 collective-permute-done.8
  316.3 0.1 collective-permute-done.7
  316.5 0.1 select_select_fusion
  316.6 0.1 slice.26
  316.7 0.8 fusion.25
  (54 shorter events, 0.2 us)
Async XLA Ops:
  7.2 247.3 %copy-start = (bf16[8192,128]{1,0:T(8,128)(2,1)S(1)}, bf16[8192,128]{1,0:T(8,128)(2,1)}, u32[]{:S(2)}) copy-start(bf16[8192,128]{1,0:T(8,128)(2,1)} %param.22) | copy-start | bytes 6291460
  7.2 224.0 %all-gather.2.cloned.1.call-start = ((), (), s32[]{:S(2)}) async-start(), calls=%async_computation | async-start | bytes 13107200 | tf_op jit(solution)/shard_map/all_gather | solution.py:95
  14.4 14.4 %copy-start.4 = (s32[640]{0:T(1024)S(1)}, s32[640]{0:T(1024)}, u32[]{:S(2)}) copy-start(s32[640]{0:T(1024)} %param.19) | copy-start | bytes 7684
  14.4 14.4 %copy-start.7 = (s32[8]{0:T(128)S(1)}, s32[8]{0:T(128)}, u32[]{:S(2)}) copy-start(s32[8]{0:T(128)} %param.18) | copy-start | bytes 100
  18.2 16.6 %collective-permute-start = (bf16[160,2048]{1,0:T(8,128)(2,1)S(1)}, bf16[160,2048]{1,0:T(8,128)(2,1)S(1)}, u32[]{:S(2)}, u32[]{:S(2)}) collective-permute-start(bf16[160,2048]{1,0:T(8,128)(2,1)S(1)} %get-tuple-element.37), channel_id=1, source_target_pairs={{0,4},{4,8},{8,12},{12,16},{16,20},{20,24},{24,28},{28,32},{32,36}... | collective-permute-start | bytes 1966088 | tf_op jit(solution)/shard_map/ppermute | solution.py:16
  20.8 32.4 %collective-permute-start.1 = (bf16[160,2048]{1,0:T(8,128)(2,1)S(1)}, bf16[160,2048]{1,0:T(8,128)(2,1)S(1)}, u32[]{:S(2)}, u32[]{:S(2)}) collective-permute-start(bf16[160,2048]{1,0:T(8,128)(2,1)S(1)} %get-tuple-element.36), channel_id=1, source_target_pairs={{0,8},{4,12},{8,16},{12,20},{16,24},{20,28},{24,32},{28,36},{32,40... | collective-permute-start | bytes 1966088 | tf_op jit(solution)/shard_map/ppermute | solution.py:16
  22.0 40.8 %collective-permute-start.2 = (bf16[160,2048]{1,0:T(8,128)(2,1)S(1)}, bf16[160,2048]{1,0:T(8,128)(2,1)S(1)}, u32[]{:S(2)}, u32[]{:S(2)}) collective-permute-start(bf16[160,2048]{1,0:T(8,128)(2,1)S(1)} %get-tuple-element.35), channel_id=1, source_target_pairs={{0,12},{4,16},{8,20},{12,24},{16,28},{20,32},{24,36},{28,40},{32,4... | collective-permute-start | bytes 1966088 | tf_op jit(solution)/shard_map/ppermute | solution.py:16
  23.5 75.9 %collective-permute-start.3 = (bf16[160,2048]{1,0:T(8,128)(2,1)S(1)}, bf16[160,2048]{1,0:T(8,128)(2,1)S(1)}, u32[]{:S(2)}, u32[]{:S(2)}) collective-permute-start(bf16[160,2048]{1,0:T(8,128)(2,1)S(1)} %get-tuple-element.34), channel_id=1, source_target_pairs={{0,16},{4,20},{8,24},{12,28},{16,32},{20,36},{24,40},{28,44},{32,4... | collective-permute-start | bytes 1966088 | tf_op jit(solution)/shard_map/ppermute | solution.py:16
  25.4 75.0 %collective-permute-start.4 = (bf16[160,2048]{1,0:T(8,128)(2,1)S(1)}, bf16[160,2048]{1,0:T(8,128)(2,1)S(1)}, u32[]{:S(2)}, u32[]{:S(2)}) collective-permute-start(bf16[160,2048]{1,0:T(8,128)(2,1)S(1)} %get-tuple-element.33), channel_id=1, source_target_pairs={{0,20},{4,24},{8,28},{12,32},{16,36},{20,40},{24,44},{28,48},{32,5... | collective-permute-start | bytes 1966088 | tf_op jit(solution)/shard_map/ppermute | solution.py:16
  34.8 74.1 %collective-permute-start.5 = (bf16[160,2048]{1,0:T(8,128)(2,1)S(1)}, bf16[160,2048]{1,0:T(8,128)(2,1)S(1)}, u32[]{:S(2)}, u32[]{:S(2)}) collective-permute-start(bf16[160,2048]{1,0:T(8,128)(2,1)S(1)} %get-tuple-element.39), channel_id=1, source_target_pairs={{0,24},{4,28},{8,32},{12,36},{16,40},{20,44},{24,48},{28,52},{32,5... | collective-permute-start | bytes 1966088 | tf_op jit(solution)/shard_map/ppermute | solution.py:16
  53.1 62.0 %collective-permute-start.6 = (bf16[160,2048]{1,0:T(8,128)(2,1)S(1)}, bf16[160,2048]{1,0:T(8,128)(2,1)S(1)}, u32[]{:S(2)}, u32[]{:S(2)}) collective-permute-start(bf16[160,2048]{1,0:T(8,128)(2,1)S(1)} %get-tuple-element.32), channel_id=1, source_target_pairs={{0,28},{4,32},{8,36},{12,40},{16,44},{20,48},{24,52},{28,56},{32,6... | collective-permute-start | bytes 1966088 | tf_op jit(solution)/shard_map/ppermute | solution.py:16
  116.0 10.1 %copy-start.6 = (f32[2048]{0:T(1024)S(1)}, f32[2048]{0:T(1024)}, u32[]{:S(2)}) copy-start(f32[2048]{0:T(1024)} %param.24) | copy-start | bytes 24580
  151.1 10.8 %copy-start.8 = (f32[64]{0:T(128)}, f32[64]{0:T(128)S(1)}, u32[]{:S(2)}) copy-start(f32[64]{0:T(128)S(1)} %multiply_power_fusion) | copy-start | bytes 772
  231.2 7.0 %copy-start.2 = (bf16[640,8192]{1,0:T(8,128)(2,1)S(1)}, bf16[640,8192]{1,0:T(8,128)(2,1)}, u32[]{:S(2)}) copy-start(bf16[640,8192]{1,0:T(8,128)(2,1)} %all-gather.2.cloned.1.call-done) | copy-start | bytes 31457284
  259.3 3.8 %copy-start.3 = (pred[640,640]{0,1:T(8,128)(4,1)S(1)}, pred[640,640]{0,1:T(8,128)(4,1)}, u32[]{:S(2)}) copy-start(pred[640,640]{0,1:T(8,128)(4,1)} %compare_and_fusion) | copy-start | bytes 1228804
  269.6 7.8 %copy-start.16 = (f32[8192]{0:T(1024)S(1)}, f32[8192]{0:T(1024)}, u32[]{:S(2)}) copy-start(f32[8192]{0:T(1024)} %param.20) | copy-start | bytes 98308
  269.6 7.8 %copy-start.18 = (f32[1024]{0:T(1024)S(1)}, f32[1024]{0:T(1024)}, u32[]{:S(2)}) copy-start(f32[1024]{0:T(1024)} %param.25) | copy-start | bytes 12292
  277.4 39.0 %copy-start.9 = (s32[8]{0:T(128)S(1)}, s32[8]{0:T(128)}, u32[]{:S(2)}) copy-start(s32[8]{0:T(128)} %param.15) | copy-start | bytes 100
  277.4 39.0 %copy-start.10 = (pred[8]{0:T(512)(128)(4,1)S(1)}, pred[8]{0:T(512)(128)(4,1)}, u32[]{:S(2)}) copy-start(pred[8]{0:T(512)(128)(4,1)} %iota_compare_fusion.3) | copy-start | bytes 28
  277.5 39.0 %copy-start.11 = (pred[8]{0:T(512)(128)(4,1)S(1)}, pred[8]{0:T(512)(128)(4,1)}, u32[]{:S(2)}) copy-start(pred[8]{0:T(512)(128)(4,1)} %iota_compare_fusion.4) | copy-start | bytes 28
  277.5 39.0 %copy-start.12 = (pred[8]{0:T(512)(128)(4,1)S(1)}, pred[8]{0:T(512)(128)(4,1)}, u32[]{:S(2)}) copy-start(pred[8]{0:T(512)(128)(4,1)} %iota_compare_fusion.5) | copy-start | bytes 28
  277.5 39.0 %copy-start.13 = (pred[8]{0:T(512)(128)(4,1)S(1)}, pred[8]{0:T(512)(128)(4,1)}, u32[]{:S(2)}) copy-start(pred[8]{0:T(512)(128)(4,1)} %iota_compare_fusion.6) | copy-start | bytes 28
  277.5 39.0 %copy-start.14 = (pred[8]{0:T(512)(128)(4,1)S(1)}, pred[8]{0:T(512)(128)(4,1)}, u32[]{:S(2)}) copy-start(pred[8]{0:T(512)(128)(4,1)} %iota_compare_fusion.7) | copy-start | bytes 28
  277.5 39.0 %copy-start.15 = (pred[8]{0:T(512)(128)(4,1)S(1)}, pred[8]{0:T(512)(128)(4,1)}, u32[]{:S(2)}) copy-start(pred[8]{0:T(512)(128)(4,1)} %iota_compare_fusion.8) | copy-start | bytes 28
  277.5 39.2 %copy-start.17 = (f32[8,160]{1,0:T(8,128)S(1)}, f32[8,160]{1,0:T(8,128)}, u32[]{:S(2)}) copy-start(f32[8,160]{1,0:T(8,128)} %param.14) | copy-start | bytes 15364
  277.5 39.1 %copy-start.19 = (s32[160]{0:T(256)S(1)}, s32[160]{0:T(256)}, u32[]{:S(2)}) copy-start(s32[160]{0:T(256)} %iota_add_fusion) | copy-start | bytes 1924
  277.5 40.0 %copy-start.1 = (bf16[8192,128]{1,0:T(8,128)(2,1)S(1)}, bf16[8192,128]{1,0:T(8,128)(2,1)}, u32[]{:S(2)}) copy-start(bf16[8192,128]{1,0:T(8,128)(2,1)} %param.22) | copy-start | bytes 6291460
  299.8 12.9 %collective-permute-start.13 = (f32[160]{0:T(256)S(1)}, f32[160]{0:T(256)S(1)}, u32[]{:S(2)}, u32[]{:S(2)}) collective-permute-start(f32[160]{0:T(256)S(1)} %get-tuple-element.52), channel_id=1, source_target_pairs={{0,124},{4,0},{8,4},{12,8},{16,12},{20,16},{24,20},{28,24},{32,28}... | collective-permute-start | bytes 1928 | tf_op jit(solution)/shard_map/ppermute | solution.py:16
  302.7 10.4 %collective-permute-start.12 = (f32[160]{0:T(256)S(1)}, f32[160]{0:T(256)S(1)}, u32[]{:S(2)}, u32[]{:S(2)}) collective-permute-start(f32[160]{0:T(256)S(1)} %get-tuple-element.51), channel_id=1, source_target_pairs={{0,120},{4,124},{8,0},{12,4},{16,8},{20,12},{24,16},{28,20},{32,24... | collective-permute-start | bytes 1928 | tf_op jit(solution)/shard_map/ppermute | solution.py:16
  308.3 6.3 %collective-permute-start.11 = (f32[160]{0:T(256)S(1)}, f32[160]{0:T(256)S(1)}, u32[]{:S(2)}, u32[]{:S(2)}) collective-permute-start(f32[160]{0:T(256)S(1)} %get-tuple-element.50), channel_id=1, source_target_pairs={{0,116},{4,120},{8,124},{12,0},{16,4},{20,8},{24,12},{28,16},{32,2... | collective-permute-start | bytes 1928 | tf_op jit(solution)/shard_map/ppermute | solution.py:16
  309.2 5.4 %collective-permute-start.10 = (f32[160]{0:T(256)S(1)}, f32[160]{0:T(256)S(1)}, u32[]{:S(2)}, u32[]{:S(2)}) collective-permute-start(f32[160]{0:T(256)S(1)} %get-tuple-element.49), channel_id=1, source_target_pairs={{0,112},{4,116},{8,120},{12,124},{16,0},{20,4},{24,8},{28,12},{32,... | collective-permute-start | bytes 1928 | tf_op jit(solution)/shard_map/ppermute | solution.py:16
  309.5 5.1 %collective-permute-start.9 = (f32[160]{0:T(256)S(1)}, f32[160]{0:T(256)S(1)}, u32[]{:S(2)}, u32[]{:S(2)}) collective-permute-start(f32[160]{0:T(256)S(1)} %get-tuple-element.48), channel_id=1, source_target_pairs={{0,108},{4,112},{8,116},{12,120},{16,124},{20,0},{24,4},{28,8},{32... | collective-permute-start | bytes 1928 | tf_op jit(solution)/shard_map/ppermute | solution.py:16
  312.6 3.7 %collective-permute-start.8 = (f32[160]{0:T(256)S(1)}, f32[160]{0:T(256)S(1)}, u32[]{:S(2)}, u32[]{:S(2)}) collective-permute-start(f32[160]{0:T(256)S(1)} %get-tuple-element.47), channel_id=1, source_target_pairs={{0,104},{4,108},{8,112},{12,116},{16,120},{20,124},{24,0},{28,4},{... | collective-permute-start | bytes 1928 | tf_op jit(solution)/shard_map/ppermute | solution.py:16
  313.1 3.3 %collective-permute-start.7 = (f32[160]{0:T(256)S(1)}, f32[160]{0:T(256)S(1)}, u32[]{:S(2)}, u32[]{:S(2)}) collective-permute-start(f32[160]{0:T(256)S(1)} %get-tuple-element.46), channel_id=1, source_target_pairs={{0,100},{4,104},{8,108},{12,112},{16,116},{20,120},{24,124},{28,0}... | collective-permute-start | bytes 1928 | tf_op jit(solution)/shard_map/ppermute | solution.py:16
  316.6 0.9 copy-start.5
Sparse Core Ops, SparseCore 0:
  130.4 100.8 all-gather.1
where the time goes:
time: 325 us; the launch traced here: 324 us
  waiting for transfers between devices  149 us (46%)
  other arithmetic  42 us (13%)
  matrix products  41.8 us (13%)
  between operations  34.6 us (11%)
  starting transfers between devices  27 us (8%)
  local copies, waits for them, and re-layouts  22.7 us (7%)
  blocking collectives  7.21 us (2%)
    ppermute x14, waiting for transfers between devices, passed_along(): lax.ppermute(value, axis, [(i, (i + by) % length) for i in range(length)])  79.7 us
    all_gather x1, waiting for transfers between devices, local(): packed = lax.all_gather(own_part, 'mp', axis=1, tiled=True)  69.3 us
    ppermute x14, starting transfers between devices, passed_along(): lax.ppermute(value, axis, [(i, (i + by) % length) for i in range(length)])  27 us
    dot_general x1, matrix products, head_values(): jnp.einsum('hgqk,khd->qhgd', weights, value_rows, preferred_element_type=...  14.9 us
    dot_general x1, matrix products, local(): queries = jnp.dot(normed, w_query, preferred_element_type=jnp.float32)  14.8 us
    gather x1, local copies, waits for them, and re-layouts, local(): own_part = jnp.take(jnp.concatenate(received, axis=0), pick_rows, axis=0)  10.1 us
    eq x8, other arithmetic, local(): slot_lanes == slot_for(shift_by)  8.29 us
    reduce_sum x1, other arithmetic, head_values(): row_total = jnp.sum(exp_scores, axis=-1, keepdims=True)  7.83 us
  transfers between devices with their start and end apart: 15, of which 9 were waited for; matrix products, arithmetic and copies ran while one was open for 7% of the time, Pallas kernels for 0%

commit v1 on v0

--- a/solution.py
+++ b/solution.py
@@ -9,6 +9,15 @@
 DISCOUNT = 0.99
 SMOOTHING = 0.95
 ROPE_BASE = 500000.0
+
+
+def sum_by_hops(x, mesh_axis):
+    size = lax.axis_size(mesh_axis)
+    total, far = (x, 1)
+    while far < size:
+        total = total + lax.ppermute(total, mesh_axis, [(i, i ^ far) for i in range(size)])
+        far = 2 * far
+    return total
 
 
 def passed_along(value, axis, by):
@@ -101,7 +110,7 @@
     values_out = jnp.dot(normed, w_value, preferred_element_type=jnp.float32)
     value_terms = head_values(queries, keys_out, values_out, segment_ids, positions, folded_head)
     value_terms = value_terms + jnp.sum(own_part.astype(jnp.float32) * value_head[None, :], axis=1)
-    packed_values = lax.psum(value_terms, "mp")
+    packed_values = sum_by_hops(value_terms, "mp")
     padded = jnp.concatenate([packed_values, jnp.zeros((slot_rows,), jnp.float32)])
     slot_values = jnp.zeros((rollouts, slot_rows), jnp.float32)
     for shift_by in range(rollouts):

time: 325 us -> 338 us (1.040)
  waiting for transfers between devices: 149 us -> 167 us
  blocking collectives: 7.21 us -> 0 us
    all_gather x1, waiting for transfers between devices: 69.3 us -> 86.6 us  [local(): packed = lax.all_gather(own_part, 'mp', axis=1, tiled=True)]
    psum x1 -> x0, blocking collectives: 7.21 us -> none  [local(): packed_values = lax.psum(value_terms, 'mp')]
    ppermute x0 -> x2, starting transfers between devices: none -> 3.72 us  [sum_by_hops(): lax.ppermute(total, mesh_axis, [(i, i ^ far) for i in range(size)])]
    unnamed x47 -> x43, local copies, waits for them, and re-layouts: 6.86 us -> 6.85 us
  transfers between devices with their start and end apart: 15 -> 17, of which waited for: 9 -> 10; matrix products, arithmetic and copies ran while one was open for 7% -> 7% of each run, Pallas kernels for 0% -> 0%
where the time goes in v1:
time: 338 us; the launch traced here: 337 us
  waiting for transfers between devices  167 us (49%)
  matrix products  41.8 us (12%)
  other arithmetic  41 us (12%)
  between operations  34.8 us (10%)
  starting transfers between devices  29.9 us (9%)
  local copies, waits for them, and re-layouts  22.7 us (7%)
    all_gather x1, waiting for transfers between devices, local(): packed = lax.all_gather(own_part, 'mp', axis=1, tiled=True)  86.6 us
    ppermute x14, waiting for transfers between devices, passed_along(): lax.ppermute(value, axis, [(i, (i + by) % length) for i in range(length)])  79.8 us
    ppermute x14, starting transfers between devices, passed_along(): lax.ppermute(value, axis, [(i, (i + by) % length) for i in range(length)])  26.1 us
    dot_general x1, matrix products, head_values(): jnp.einsum('hgqk,khd->qhgd', weights, value_rows, preferred_element_type=...  14.9 us
    dot_general x1, matrix products, local(): queries = jnp.dot(normed, w_query, preferred_element_type=jnp.float32)  14.8 us
    gather x1, local copies, waits for them, and re-layouts, local(): own_part = jnp.take(jnp.concatenate(received, axis=0), pick_rows, axis=0)  10.1 us
    reduce_sum x1, other arithmetic, head_values(): row_total = jnp.sum(exp_scores, axis=-1, keepdims=True)  7.83 us
    eq x8, other arithmetic, local(): slot_lanes == slot_for(shift_by)  7.19 us
  transfers between devices with their start and end apart: 17, of which 10 were waited for; matrix products, arithmetic and copies ran while one was open for 7% of the time, Pallas kernels for 0%

profile of v1, /device:TPU:1, one launch (start us, length us, event | category | flops | bytes accessed | tf_op | source)
XLA Modules:
  0.0 337.1 jit_solution(8515653503310208259)
XLA Ops:
  7.4 1.9 fusion.49
  14.4 3.8 %constant_dynamic-slice_fusion = (bf16[160,2048]{1,0:T(8,128)(2,1)S(1)}, bf16[160,2048]{1,0:T(8,128)(2,1)S(1)}, bf16[160,2048]{1,0:T(8,128)(2,1)S(1)}, bf16[160,...) fusion(bf16[1280,2048]{1,0:T(8,128)(2,1)} %param.13, ...), kind=kLoop, calls=%fused_computation.98 | loop fusion | bytes 10485792 | tf_op jit(solution)/shard_map/dynamic_slice | solution.py:92
  18.2 2.6 collective-permute-start
  20.8 1.2 collective-permute-start.1
  22.0 1.5 collective-permute-start.2
  23.6 1.9 collective-permute-start.3
  25.4 3.4 %collective-permute-start.4 = (bf16[160,2048]{1,0:T(8,128)(2,1)S(1)}, bf16[160,2048]{1,0:T(8,128)(2,1)S(1)}, u32[]{:S(2)}, u32[]{:S(2)}) collective-permute-start(bf16[160,2048]{1,0:T(8,128)(2,1)S(1)} %get-tuple-element.33), channel_id=1, source_target_pairs={{0,20},{4,24},{8,28},{12,32},{16,36},{20,40},{24,44},{28,48},{32,5... | collective-permute-start | bytes 1966088 | tf_op jit(solution)/shard_map/ppermute | solution.py:25
  28.8 0.1 select_reduce_fusion.1
  29.0 5.8 %collective-permute-done = bf16[160,2048]{1,0:T(8,128)(2,1)S(1)} collective-permute-done((bf16[160,2048]{1,0:T(8,128)(2,1)S(1)}, bf16[160,2048]{1,0:T(8,128)(2,1)S(1)}, u32[]{:S(2)}, u32[]{:S(2)}) %collective-permute-start) | collective-permute-done | bytes 655392 | tf_op jit(solution)/shard_map/ppermute | solution.py:25
  34.8 2.8 collective-permute-start.5
  37.6 0.9 constant_dynamic-update-slice_fusion.6
  38.5 14.7 %collective-permute-done.1 = bf16[160,2048]{1,0:T(8,128)(2,1)S(1)} collective-permute-done((bf16[160,2048]{1,0:T(8,128)(2,1)S(1)}, bf16[160,2048]{1,0:T(8,128)(2,1)S(1)}, u32[]{:S(2)}, u32[]{:S(2)}) %collective-permute-start.1) | collective-permute-done | bytes 655392 | tf_op jit(solution)/shard_map/ppermute | solution.py:25
  53.2 0.9 constant_dynamic-update-slice_fusion.5
  54.1 8.8 %collective-permute-done.2 = bf16[160,2048]{1,0:T(8,128)(2,1)S(1)} collective-permute-done((bf16[160,2048]{1,0:T(8,128)(2,1)S(1)}, bf16[160,2048]{1,0:T(8,128)(2,1)S(1)}, u32[]{:S(2)}, u32[]{:S(2)}) %collective-permute-start.2) | collective-permute-done | bytes 655392 | tf_op jit(solution)/shard_map/ppermute | solution.py:25
  62.9 0.9 constant_dynamic-update-slice_fusion.4
  63.8 35.7 %collective-permute-done.3 = bf16[160,2048]{1,0:T(8,128)(2,1)S(1)} collective-permute-done((bf16[160,2048]{1,0:T(8,128)(2,1)S(1)}, bf16[160,2048]{1,0:T(8,128)(2,1)S(1)}, u32[]{:S(2)}, u32[]{:S(2)}) %collective-permute-start.3) | collective-permute-done | bytes 655392 | tf_op jit(solution)/shard_map/ppermute | solution.py:25
  99.5 0.9 constant_dynamic-update-slice_fusion.3
  100.4 0.9 constant_dynamic-update-slice_fusion.2
  101.3 7.6 %collective-permute-done.5 = bf16[160,2048]{1,0:T(8,128)(2,1)S(1)} collective-permute-done((bf16[160,2048]{1,0:T(8,128)(2,1)S(1)}, bf16[160,2048]{1,0:T(8,128)(2,1)S(1)}, u32[]{:S(2)}, u32[]{:S(2)}) %collective-permute-start.5) | collective-permute-done | bytes 655392 | tf_op jit(solution)/shard_map/ppermute | solution.py:25
  108.9 0.9 constant_dynamic-update-slice_fusion.1
  109.8 5.4 %collective-permute-done.6 = bf16[160,2048]{1,0:T(8,128)(2,1)S(1)} collective-permute-done((bf16[160,2048]{1,0:T(8,128)(2,1)S(1)}, bf16[160,2048]{1,0:T(8,128)(2,1)S(1)}, u32[]{:S(2)}, u32[]{:S(2)}) %collective-permute-start.6) | collective-permute-done | bytes 655392 | tf_op jit(solution)/shard_map/ppermute | solution.py:25
  115.2 0.9 constant_dynamic-update-slice_fusion
  116.1 10.1 %gather_fusion = bf16[640,2048]{1,0:T(8,128)(2,1)} fusion(bf16[1280,2048]{1,0:T(8,128)(2,1)} %constant_dynamic-update-slice_fusion, s32[1024]{0:T(1024)S(1)} %pad_clamp_fusion), kind=kCustom, calls=%fused_computation | custom fusion | bytes 5245440 | tf_op jit(solution)/shard_map/jit(_take)/gather | solution.py:103
  126.2 4.1 %multiply_reduce_fusion = (f32[640]{0:T(1024)S(1)}, bf16[640,2048]{1,0:T(8,128)(2,1)}) fusion(f32[2048]{0:T(1024)S(1)} %copy-done.6, bf16[640,2048]{1,0:T(8,128)(2,1)} %gather_fusion, pred[640]{0:T(1024)(128)(4,1)S(1)} %compare_and_fusion.1), kind=kLoop, calls=%fused_computation.13 | loop fusion | flops 5242240 | bytes 5254272 | tf_op jit(solution)/shard_map/reduce_sum | solution.py:112
  130.3 1.2 iota_compare_fusion.3
  131.5 1.2 iota_compare_fusion.4
  132.7 1.1 iota_compare_fusion.5
  133.8 1.2 iota_compare_fusion.6
  135.0 0.6 iota_add_fusion
  135.5 5.9 %fusion.58 = (s32[]{:T(128)}, s32[]{:T(128)}, s32[]{:T(128)}, s32[]{:T(128)}, s32[]{:T(128)}, /*index=5*/s32[]{:T(128)}, s32[]{:T(128)}, s32[]{:T(128)}) fusion(s32[8]{0:T(128)S(1)} %copy-done.7, s32[]{:T(128)} %get-tuple-element.67, s32[]{:T(128)} %get-tuple-element.66, s32[]{:T(128)} %get-tuple-element.65, s32[]{:T(128)} %get-tuple-element.64, ...), kind=kLoop, calls=%fused_computation.140 | loop fusion | flops 184 | bytes 96 | tf_op jit(solution)/shard_map/reduce_sum | solution.py:119
  141.4 1.1 compare_and_fusion
  142.6 2.0 multiply_cosine_fusion
  144.6 86.6 %all-gather.2.cloned.1.call-done = bf16[640,8192]{1,0:T(8,128)(2,1)} async-done(((bf16[640,2048]{1,0:T(8,128)(2,1)}), bf16[640,8192]{1,0:T(8,128)(2,1)}) %all-gather.2.cloned.1.call-update) | async-done | bytes 10485776 | tf_op jit(solution)/shard_map/all_gather | solution.py:104
  231.3 6.2 %fusion = f32[640]{0:T(1024)S(1)} fusion(bf16[640,8192]{1,0:T(8,128)(2,1)} %all-gather.2.cloned.1.call-done), kind=kLoop, calls=%fused_computation.3 | loop fusion | flops 15728000 | bytes 10488320 | tf_op jit(solution)/shard_map/reduce_sum | solution.py:106
  237.5 0.7 copy-done.2
  238.2 14.8 %convolution_bitcast_fusion = f32[80,8,8,128]{3,1,2,0:T(8,128)S(1)} fusion(bf16[8192,1024]{1,0:T(8,128)(2,1)} %param.21, bf16[640,8192]{1,0:T(8,128)(2,1)S(1)} %copy-done.2, f32[8192]{0:T(1024)} %param.20, f32[640]{0:T(1024)S(1)} %add_rsqrt_fusion), kind=kOutput, calls=%fused_computation.19 | convolution fusion | flops 10758389760 | bytes 29919744 | tf_op jit(solution)/shard_map/dot_general | solution.py:108
  253.1 0.6 copy.35
  253.7 0.8 fusion.86
  254.5 4.9 %convolution_bitcast_fusion.1 = f32[640,1,128]{0,2,1:T(8,128)} fusion(bf16[8192,128]{1,0:T(8,128)(2,1)S(1)} %copy-done, bf16[640,8192]{1,0:T(8,128)(2,1)S(1)} %copy-done.2, f32[8192]{0:T(1024)} %param.20, f32[640]{0:T(1024)S(1)} %add_rsqrt_fusion), kind=kOutput, calls=%fused_computation.25 | convolution fusion | flops 1363148800 | bytes 12945920 | tf_op jit(solution)/shard_map/dot_general | solution.py:109
  259.4 1.7 fusion.36
  261.1 2.1 subtract_convert_fusion
  263.2 6.4 %fusion.3 = (f32[8,640]{1,0:T(8,128)S(1)}, f32[640,640,8]{1,0,2:T(8,128)}) fusion(pred[640,640]{0,1:T(8,128)(4,1)S(1)} %copy-done.3, bf16[640,8,64]{2,0,1:T(8,128)(2,1)S(1)} %get-tuple-element.31, bf16[640,8,64]{2,0,1:T(8,128)(2,1)S(1)} %get-tuple-element.30, bf16[640,64]{0,1:T(8,128)(2,1)S(1)} %get-tuple-element.43, bf16[640,64]{0,1:T(8,128)(2,1)S(1)} %get-tuple-element.42), kind=kOutput, calls=%fused_computation.9 | convolution fusion | flops 851635200 | bytes 15011840 | tf_op jit(solution)/shard_map/qhgd,khd->hgqk/dot_general | solution.py:52
  269.6 7.8 %fusion.4 = f32[8,640]{1,0:T(8,128)S(1)} fusion(f32[640,640,8]{1,0,2:T(8,128)} %get-tuple-element.58, f32[8,640]{1,0:T(8,128)S(1)} %get-tuple-element.57, pred[640,640]{0,1:T(8,128)(4,1)S(1)} %copy-done.3), kind=kLoop, calls=%fused_computation.10 | loop fusion | flops 16378880 | bytes 13557760 | tf_op jit(solution)/shard_map/reduce_sum | solution.py:59
  277.6 14.9 %fusion.7 = f32[640]{0:T(1024)S(1)} fusion(f32[8,640]{1,0:T(8,128)S(1)} %fusion.4, f32[8,640]{1,0:T(8,128)S(1)} %get-tuple-element.57, f32[640,640,8]{1,0,2:T(8,128)} %get-tuple-element.58, pred[640,640]{0,1:T(8,128)(4,1)S(1)} %copy-done.3, f32[8,128]{1,0:T(8,128)S(1)} %bitcast.51, bf16[8192,128]{1,0:T(8,128)(2,1)} %param.23, ...), kind=kOutput, calls=%fused_computation.15 | convolution fusion | flops 2223062528 | bytes 26182656 | tf_op jit(solution)/shard_map/hgqk,khd->qhgd/dot_general | solution.py:61
  292.5 1.3 collective-permute-start.7
  293.8 0.7 iota_compare_fusion.7
  294.5 0.6 collective-permute-done.7
  295.0 2.4 collective-permute-start.8
  297.5 0.6 iota_compare_fusion.8
  313.2 0.1 pad_dynamic-slice_fusion.7
  313.4 2.3 collective-permute-start.15
  315.7 4.8 %collective-permute-start.14 = (f32[160]{0:T(256)S(1)}, f32[160]{0:T(256)S(1)}, u32[]{:S(2)}, u32[]{:S(2)}) collective-permute-start(f32[160]{0:T(256)S(1)} %get-tuple-element.51), channel_id=1, source_target_pairs={{0,120},{4,124},{8,0},{12,4},{16,8},{20,12},{24,16},{28,20},{32,24... | collective-permute-start | bytes 1928 | tf_op jit(solution)/shard_map/ppermute | solution.py:25
  320.5 0.6 iota_compare_fusion.9
  321.0 0.9 collective-permute-start.13
  321.9 0.9 collective-permute-start.12
  322.8 2.6 collective-permute-start.11
  325.4 0.5 collective-permute-start.10
  325.9 0.8 collective-permute-start.9
  326.6 0.6 iota_compare_fusion.10
  327.3 1.7 collective-permute-done.10
  329.0 0.1 collective-permute-done.9
  329.2 0.1 select_select_fusion
  329.3 0.1 slice.26
  329.4 0.8 fusion.25
  (55 shorter events, 0.3 us)
Async XLA Ops:
  7.2 247.3 %copy-start = (bf16[8192,128]{1,0:T(8,128)(2,1)S(1)}, bf16[8192,128]{1,0:T(8,128)(2,1)}, u32[]{:S(2)}) copy-start(bf16[8192,128]{1,0:T(8,128)(2,1)} %param.22) | copy-start | bytes 6291460
  7.2 224.1 %all-gather.2.cloned.1.call-start = ((), (), s32[]{:S(2)}) async-start(), calls=%async_computation | async-start | bytes 13107200 | tf_op jit(solution)/shard_map/all_gather | solution.py:104
  14.4 14.4 %copy-start.4 = (s32[640]{0:T(1024)S(1)}, s32[640]{0:T(1024)}, u32[]{:S(2)}) copy-start(s32[640]{0:T(1024)} %param.19) | copy-start | bytes 7684
  14.4 14.4 %copy-start.7 = (s32[8]{0:T(128)S(1)}, s32[8]{0:T(128)}, u32[]{:S(2)}) copy-start(s32[8]{0:T(128)} %param.18) | copy-start | bytes 100
  18.2 16.6 %collective-permute-start = (bf16[160,2048]{1,0:T(8,128)(2,1)S(1)}, bf16[160,2048]{1,0:T(8,128)(2,1)S(1)}, u32[]{:S(2)}, u32[]{:S(2)}) collective-permute-start(bf16[160,2048]{1,0:T(8,128)(2,1)S(1)} %get-tuple-element.37), channel_id=1, source_target_pairs={{0,4},{4,8},{8,12},{12,16},{16,20},{20,24},{24,28},{28,32},{32,36}... | collective-permute-start | bytes 1966088 | tf_op jit(solution)/shard_map/ppermute | solution.py:25
  20.8 32.4 %collective-permute-start.1 = (bf16[160,2048]{1,0:T(8,128)(2,1)S(1)}, bf16[160,2048]{1,0:T(8,128)(2,1)S(1)}, u32[]{:S(2)}, u32[]{:S(2)}) collective-permute-start(bf16[160,2048]{1,0:T(8,128)(2,1)S(1)} %get-tuple-element.36), channel_id=1, source_target_pairs={{0,8},{4,12},{8,16},{12,20},{16,24},{20,28},{24,32},{28,36},{32,40... | collective-permute-start | bytes 1966088 | tf_op jit(solution)/shard_map/ppermute | solution.py:25
  22.0 40.8 %collective-permute-start.2 = (bf16[160,2048]{1,0:T(8,128)(2,1)S(1)}, bf16[160,2048]{1,0:T(8,128)(2,1)S(1)}, u32[]{:S(2)}, u32[]{:S(2)}) collective-permute-start(bf16[160,2048]{1,0:T(8,128)(2,1)S(1)} %get-tuple-element.35), channel_id=1, source_target_pairs={{0,12},{4,16},{8,20},{12,24},{16,28},{20,32},{24,36},{28,40},{32,4... | collective-permute-start | bytes 1966088 | tf_op jit(solution)/shard_map/ppermute | solution.py:25
  23.6 75.9 %collective-permute-start.3 = (bf16[160,2048]{1,0:T(8,128)(2,1)S(1)}, bf16[160,2048]{1,0:T(8,128)(2,1)S(1)}, u32[]{:S(2)}, u32[]{:S(2)}) collective-permute-start(bf16[160,2048]{1,0:T(8,128)(2,1)S(1)} %get-tuple-element.34), channel_id=1, source_target_pairs={{0,16},{4,20},{8,24},{12,28},{16,32},{20,36},{24,40},{28,44},{32,4... | collective-permute-start | bytes 1966088 | tf_op jit(solution)/shard_map/ppermute | solution.py:25
  25.4 75.0 %collective-permute-start.4 = (bf16[160,2048]{1,0:T(8,128)(2,1)S(1)}, bf16[160,2048]{1,0:T(8,128)(2,1)S(1)}, u32[]{:S(2)}, u32[]{:S(2)}) collective-permute-start(bf16[160,2048]{1,0:T(8,128)(2,1)S(1)} %get-tuple-element.33), channel_id=1, source_target_pairs={{0,20},{4,24},{8,28},{12,32},{16,36},{20,40},{24,44},{28,48},{32,5... | collective-permute-start | bytes 1966088 | tf_op jit(solution)/shard_map/ppermute | solution.py:25
  34.8 74.1 %collective-permute-start.5 = (bf16[160,2048]{1,0:T(8,128)(2,1)S(1)}, bf16[160,2048]{1,0:T(8,128)(2,1)S(1)}, u32[]{:S(2)}, u32[]{:S(2)}) collective-permute-start(bf16[160,2048]{1,0:T(8,128)(2,1)S(1)} %get-tuple-element.39), channel_id=1, source_target_pairs={{0,24},{4,28},{8,32},{12,36},{16,40},{20,44},{24,48},{28,52},{32,5... | collective-permute-start | bytes 1966088 | tf_op jit(solution)/shard_map/ppermute | solution.py:25
  53.2 62.0 %collective-permute-start.6 = (bf16[160,2048]{1,0:T(8,128)(2,1)S(1)}, bf16[160,2048]{1,0:T(8,128)(2,1)S(1)}, u32[]{:S(2)}, u32[]{:S(2)}) collective-permute-start(bf16[160,2048]{1,0:T(8,128)(2,1)S(1)} %get-tuple-element.32), channel_id=1, source_target_pairs={{0,28},{4,32},{8,36},{12,40},{16,44},{20,48},{24,52},{28,56},{32,6... | collective-permute-start | bytes 1966088 | tf_op jit(solution)/shard_map/ppermute | solution.py:25
  116.1 10.1 %copy-start.6 = (f32[2048]{0:T(1024)S(1)}, f32[2048]{0:T(1024)}, u32[]{:S(2)}) copy-start(f32[2048]{0:T(1024)} %param.24) | copy-start | bytes 24580
  130.3 14.3 %copy-start.8 = (f32[64]{0:T(128)}, f32[64]{0:T(128)S(1)}, u32[]{:S(2)}) copy-start(f32[64]{0:T(128)S(1)} %multiply_power_fusion) | copy-start | bytes 772
  231.3 7.0 %copy-start.2 = (bf16[640,8192]{1,0:T(8,128)(2,1)S(1)}, bf16[640,8192]{1,0:T(8,128)(2,1)}, u32[]{:S(2)}) copy-start(bf16[640,8192]{1,0:T(8,128)(2,1)} %all-gather.2.cloned.1.call-done) | copy-start | bytes 31457284
  259.4 3.8 %copy-start.3 = (pred[640,640]{0,1:T(8,128)(4,1)S(1)}, pred[640,640]{0,1:T(8,128)(4,1)}, u32[]{:S(2)}) copy-start(pred[640,640]{0,1:T(8,128)(4,1)} %compare_and_fusion) | copy-start | bytes 1228804
  269.6 7.8 %copy-start.14 = (f32[8192]{0:T(1024)S(1)}, f32[8192]{0:T(1024)}, u32[]{:S(2)}) copy-start(f32[8192]{0:T(1024)} %param.20) | copy-start | bytes 98308
  269.6 7.8 %copy-start.16 = (f32[1024]{0:T(1024)S(1)}, f32[1024]{0:T(1024)}, u32[]{:S(2)}) copy-start(f32[1024]{0:T(1024)} %param.25) | copy-start | bytes 12292
  277.5 51.7 %copy-start.9 = (s32[8]{0:T(128)S(1)}, s32[8]{0:T(128)}, u32[]{:S(2)}) copy-start(s32[8]{0:T(128)} %param.15) | copy-start | bytes 100
  277.5 51.7 %copy-start.10 = (pred[8]{0:T(512)(128)(4,1)S(1)}, pred[8]{0:T(512)(128)(4,1)}, u32[]{:S(2)}) copy-start(pred[8]{0:T(512)(128)(4,1)} %iota_compare_fusion.3) | copy-start | bytes 28
  277.5 51.7 %copy-start.11 = (pred[8]{0:T(512)(128)(4,1)S(1)}, pred[8]{0:T(512)(128)(4,1)}, u32[]{:S(2)}) copy-start(pred[8]{0:T(512)(128)(4,1)} %iota_compare_fusion.4) | copy-start | bytes 28
  277.5 51.7 %copy-start.12 = (pred[8]{0:T(512)(128)(4,1)S(1)}, pred[8]{0:T(512)(128)(4,1)}, u32[]{:S(2)}) copy-start(pred[8]{0:T(512)(128)(4,1)} %iota_compare_fusion.5) | copy-start | bytes 28
  277.5 51.7 %copy-start.13 = (pred[8]{0:T(512)(128)(4,1)S(1)}, pred[8]{0:T(512)(128)(4,1)}, u32[]{:S(2)}) copy-start(pred[8]{0:T(512)(128)(4,1)} %iota_compare_fusion.6) | copy-start | bytes 28
  277.5 51.9 %copy-start.15 = (f32[8,160]{1,0:T(8,128)S(1)}, f32[8,160]{1,0:T(8,128)}, u32[]{:S(2)}) copy-start(f32[8,160]{1,0:T(8,128)} %param.14) | copy-start | bytes 15364
  277.5 51.8 %copy-start.17 = (s32[160]{0:T(256)S(1)}, s32[160]{0:T(256)}, u32[]{:S(2)}) copy-start(s32[160]{0:T(256)} %iota_add_fusion) | copy-start | bytes 1924
  277.6 52.7 %copy-start.1 = (bf16[8192,128]{1,0:T(8,128)(2,1)S(1)}, bf16[8192,128]{1,0:T(8,128)(2,1)}, u32[]{:S(2)}) copy-start(bf16[8192,128]{1,0:T(8,128)(2,1)} %param.22) | copy-start | bytes 6291460
  292.5 2.5 collective-permute-start.7
  295.0 18.2 %collective-permute-start.8 = (f32[640]{0:T(1024)S(1)}, f32[640]{0:T(1024)S(1)}, u32[]{:S(2)}, u32[]{:S(2)}) collective-permute-start(f32[640]{0:T(1024)S(1)} %add.257), channel_id=1, source_target_pairs={{0,2},{1,3},{2,0},{3,1},{4,6},{5,7},{6,4},{7,5},{8,10},{9,11},{10,... | collective-permute-start | bytes 7688 | tf_op jit(solution)/shard_map/ppermute | solution.py:18
  313.4 12.0 %collective-permute-start.15 = (f32[160]{0:T(256)S(1)}, f32[160]{0:T(256)S(1)}, u32[]{:S(2)}, u32[]{:S(2)}) collective-permute-start(f32[160]{0:T(256)S(1)} %get-tuple-element.52), channel_id=1, source_target_pairs={{0,124},{4,0},{8,4},{12,8},{16,12},{20,16},{24,20},{28,24},{32,28}... | collective-permute-start | bytes 1928 | tf_op jit(solution)/shard_map/ppermute | solution.py:25
  315.7 10.2 %collective-permute-start.14 = (f32[160]{0:T(256)S(1)}, f32[160]{0:T(256)S(1)}, u32[]{:S(2)}, u32[]{:S(2)}) collective-permute-start(f32[160]{0:T(256)S(1)} %get-tuple-element.51), channel_id=1, source_target_pairs={{0,120},{4,124},{8,0},{12,4},{16,8},{20,12},{24,16},{28,20},{32,24... | collective-permute-start | bytes 1928 | tf_op jit(solution)/shard_map/ppermute | solution.py:25
  321.0 6.3 %collective-permute-start.13 = (f32[160]{0:T(256)S(1)}, f32[160]{0:T(256)S(1)}, u32[]{:S(2)}, u32[]{:S(2)}) collective-permute-start(f32[160]{0:T(256)S(1)} %get-tuple-element.50), channel_id=1, source_target_pairs={{0,116},{4,120},{8,124},{12,0},{16,4},{20,8},{24,12},{28,16},{32,2... | collective-permute-start | bytes 1928 | tf_op jit(solution)/shard_map/ppermute | solution.py:25
  321.9 5.4 %collective-permute-start.12 = (f32[160]{0:T(256)S(1)}, f32[160]{0:T(256)S(1)}, u32[]{:S(2)}, u32[]{:S(2)}) collective-permute-start(f32[160]{0:T(256)S(1)} %get-tuple-element.49), channel_id=1, source_target_pairs={{0,112},{4,116},{8,120},{12,124},{16,0},{20,4},{24,8},{28,12},{32,... | collective-permute-start | bytes 1928 | tf_op jit(solution)/shard_map/ppermute | solution.py:25
  322.8 4.5 %collective-permute-start.11 = (f32[160]{0:T(256)S(1)}, f32[160]{0:T(256)S(1)}, u32[]{:S(2)}, u32[]{:S(2)}) collective-permute-start(f32[160]{0:T(256)S(1)} %get-tuple-element.48), channel_id=1, source_target_pairs={{0,108},{4,112},{8,116},{12,120},{16,124},{20,0},{24,4},{28,8},{32... | collective-permute-start | bytes 1928 | tf_op jit(solution)/shard_map/ppermute | solution.py:25
  325.4 3.7 %collective-permute-start.10 = (f32[160]{0:T(256)S(1)}, f32[160]{0:T(256)S(1)}, u32[]{:S(2)}, u32[]{:S(2)}) collective-permute-start(f32[160]{0:T(256)S(1)} %get-tuple-element.47), channel_id=1, source_target_pairs={{0,104},{4,108},{8,112},{12,116},{16,120},{20,124},{24,0},{28,4},{... | collective-permute-start | bytes 1928 | tf_op jit(solution)/shard_map/ppermute | solution.py:25
  325.9 3.3 collective-permute-start.9
  329.3 0.9 copy-start.5
Sparse Core Ops, SparseCore 0:
  130.4 100.8 all-gather.1
